TPU v7x, 512 devices: a whole 4x4x16 slice. The times are simulated.
512 devices in a mesh: cells: 64 (over z, x), sub: 8 (over y, core).
Axes of the slice: x: 4, y: 4, z: 16, core: 2. Of those that a mesh axis runs over, the one named last changes fastest.
Arguments:
- snapshots: float32 [262144, 256], P(('cells', 'sub')), may hold values from -10 to 10, as said below
- volumes: float32 [262144], P(('cells', 'sub')), may hold values from 0.1 to 10
- live_rows: int32 [512], P(('cells', 'sub')), may hold values from 256 to 512, as said below
- probes: float32 [64, 262144], P(None, ('cells', 'sub')), may hold values from -6 to 6
Outputs:
- basis: float32 [262144, 256], P(('cells', 'sub'))
- factor: float32 [256, 256], replicated
- coefficients: float32 [64, 256], replicated
Inputs may be any that keep to these rules, and one draw needn't show every extreme that they name: `live_rows`: each entry is the live row count of one device's block of 512 row slots; live rows come first in the block. Some device has all 512 live, some has 256. `snapshots`: the columns are linearly independent.
All inputs are finite; a program needn't handle non-finite values.
Results may differ from a plain program's by a relative error of at most 0.00013.
Values sent between devices are 32-bit elements; how exact they have to be, the bound alone decides.
A program may use at most 64 MiB of HBM per device.

v0:
```python
import jax
import jax.numpy as jnp
from jax import lax
from jax.sharding import PartitionSpec as P

HIGHEST = lax.Precision.HIGHEST


def reduce_all(terms):
    return lax.psum((terms[0],), ("cells", "sub"))


def matmul(left, right):
    return jnp.dot(left, right, precision=HIGHEST, preferred_element_type=jnp.float32)


def small_cholesky(block):
    width = block.shape[0]
    positions = lax.iota(jnp.int32, width)

    def column_step(index, lower):
        unit = (positions == index).astype(jnp.float32)
        column = matmul(block, unit)
        lower_row = matmul(unit, lower)
        remain = column - matmul(lower, lower_row)
        pivot = jnp.sqrt(jnp.sum(remain * unit))
        filled = jnp.where(positions >= index, remain / pivot, jnp.float32(0.0))
        return lower + filled[:, None] * unit[None, :]

    return lax.fori_loop(0, width, column_step, jnp.zeros((width, width), jnp.float32))


def small_lower_inverse(lower):
    width = lower.shape[0]
    positions = lax.iota(jnp.int32, width)

    def row_step(index, result):
        unit = (positions == index).astype(jnp.float32)
        lower_row = matmul(unit, lower)
        pivot = jnp.sum(lower_row * unit)
        before = jnp.where(positions < index, lower_row, jnp.float32(0.0))
        solved = (unit - matmul(before, result)) / pivot
        return result + unit[:, None] * solved[None, :]

    return lax.fori_loop(0, width, row_step, jnp.zeros((width, width), jnp.float32))


def factorize(gram_matrix):
    order = gram_matrix.shape[0]
    block = 16
    count = order // block
    working = gram_matrix
    lower_full = jnp.zeros((order, order), jnp.float32)
    diagonal_inverses = []
    for outer in range(count):
        start = outer * block
        finish = start + block
        lower_block = small_cholesky(working[start:finish, start:finish])
        inverse_block = small_lower_inverse(lower_block)
        diagonal_inverses.append(inverse_block)
        lower_full = lower_full.at[start:finish, start:finish].set(lower_block)
        if finish < order:
            panel = matmul(working[finish:, start:finish], inverse_block.T)
            lower_full = lower_full.at[finish:, start:finish].set(panel)
            trailing = working[finish:, finish:] - lax.dot_general(
                panel,
                panel,
                (((1,), (1,)), ((), ())),
                precision=HIGHEST,
                preferred_element_type=jnp.float32,
            )
            working = working.at[finish:, finish:].set(trailing)
    lower_inverse = jnp.zeros((order, order), jnp.float32)
    for outer in range(count):
        start = outer * block
        finish = start + block
        lower_inverse = lower_inverse.at[start:finish, start:finish].set(diagonal_inverses[outer])
        for inner in range(outer):
            begin = inner * block
            mixed = matmul(
                lower_full[start:finish, begin:start],
                lower_inverse[begin:start, begin : begin + block],
            )
            lower_inverse = lower_inverse.at[start:finish, begin : begin + block].set(
                -matmul(diagonal_inverses[outer], mixed)
            )
    return (lower_full.T, lower_inverse.T)


def per_device(snapshots, volumes, live_rows, probes):
    row_count = snapshots.shape[0]
    total_rows = row_count * lax.axis_size("cells") * lax.axis_size("sub")
    root_total = jnp.sqrt(jnp.float32(total_rows))
    live_mask = lax.iota(jnp.int32, row_count) < live_rows[0]
    row_scale = jnp.where(live_mask, jnp.sqrt(volumes), jnp.float32(0.0))
    weighted = snapshots * row_scale[:, None]
    probe_weighted = probes * row_scale[None, :]
    gram_local = lax.dot_general(
        weighted,
        weighted,
        (((0,), (0,)), ((), ())),
        precision=HIGHEST,
        preferred_element_type=jnp.float32,
    ) / jnp.float32(total_rows)
    gram_matrix = reduce_all((gram_local,))[0]
    factor, inverse = factorize(gram_matrix)
    basis_block = jnp.dot(weighted, inverse, precision=HIGHEST, preferred_element_type=jnp.float32)
    projected = (
        jnp.dot(probe_weighted, basis_block, precision=HIGHEST, preferred_element_type=jnp.float32)
        / root_total
    )
    coefficients = reduce_all((projected,))[0]
    return (basis_block, factor, coefficients)


def solution(mesh):
    placed = (
        P(("cells", "sub"), None),
        P(("cells", "sub")),
        P(("cells", "sub")),
        P(None, ("cells", "sub")),
    )
    return jax.shard_map(
        per_device,
        mesh=mesh,
        in_specs=placed,
        out_specs=(P(("cells", "sub"), None), P(), P()),
        check_vma=False,
    )
```

profile of v0, /device:TPU:1, one launch (start us, length us, event | category | flops | bytes accessed | tf_op | source)
XLA Modules:
  0.0 2039.3 jit_solution(2724257691002852006)
XLA Ops:
  11.3 472.3 %all-reduce.5.cloned.1.call-done = f32[256,256]{1,0:T(8,128)} async-done(((f32[256,256]{1,0:T(8,128)}), f32[256,256]{1,0:T(8,128)}) %all-reduce.5.cloned.1.call-update) | async-done | bytes 262160 | tf_op jit(solution)/shard_map/psum | solution.py:10
  484.3 28.8 %while.662 = (s32[]{:T(128)}, f32[16,16]{1,0:T(8,128)S(1)}, f32[16,16]{1,0:T(8,128)S(1)}, s32[]{:T(128)}, s32[]{:T(128)}) while((s32[]{:T(128)}, f32[16,16]{1,0:T(8,128)S(1)}, f32[16,16]{1,0:T(8,128)S(1)}, s32[]{:T(128)}, s32[]{:T(128)}) %tuple.1794), condition=%wide.region_3.4_spmd.clone.clone, body=%wide.region_1.3_spmd.clone.clone.sunk | while | flops 10674 | bytes 5869 | solution.py:30
  513.2 25.4 %while.663 = (s32[]{:T(128)}, f32[16,16]{1,0:T(8,128)S(1)}, f32[16,16]{1,0:T(8,128)S(1)}, s32[]{:T(128)}, s32[]{:T(128)}) while((s32[]{:T(128)}, f32[16,16]{1,0:T(8,128)S(1)}, f32[16,16]{1,0:T(8,128)S(1)}, s32[]{:T(128)}, s32[]{:T(128)}) %tuple.1797), condition=%wide.region_6.7_spmd.clone.clone, body=%wide.region_4.6_spmd.clone.clone.sunk | while | flops 7362 | bytes 4572 | solution.py:45
  540.2 28.8 %while.664 = (s32[]{:T(128)}, f32[16,16]{1,0:T(8,128)S(1)}, f32[16,16]{1,0:T(8,128)S(1)}, s32[]{:T(128)}, s32[]{:T(128)}) while((s32[]{:T(128)}, f32[16,16]{1,0:T(8,128)S(1)}, f32[16,16]{1,0:T(8,128)S(1)}, s32[]{:T(128)}, s32[]{:T(128)}) %tuple.1800), condition=%wide.region_9.10_spmd.clone.clone, body=%wide.region_7.9_spmd.clone.clone.sunk | while | flops 10674 | bytes 5869 | solution.py:30
  569.0 25.4 %while.665 = (s32[]{:T(128)}, f32[16,16]{1,0:T(8,128)S(1)}, f32[16,16]{1,0:T(8,128)S(1)}, s32[]{:T(128)}, s32[]{:T(128)}) while((s32[]{:T(128)}, f32[16,16]{1,0:T(8,128)S(1)}, f32[16,16]{1,0:T(8,128)S(1)}, s32[]{:T(128)}, s32[]{:T(128)}) %tuple.1803), condition=%wide.region_12.13_spmd.clone.clone, body=%wide.region_10.12_spmd.clone.clone.sunk | while | flops 7362 | bytes 4572 | solution.py:45
  595.2 28.8 %while.666 = (s32[]{:T(128)}, f32[16,16]{1,0:T(8,128)S(1)}, f32[16,16]{1,0:T(8,128)S(1)}, s32[]{:T(128)}, s32[]{:T(128)}) while((s32[]{:T(128)}, f32[16,16]{1,0:T(8,128)S(1)}, f32[16,16]{1,0:T(8,128)S(1)}, s32[]{:T(128)}, s32[]{:T(128)}) %tuple.1806), condition=%wide.region_15.16_spmd.clone.clone, body=%wide.region_13.15_spmd.clone.clone.sunk | while | flops 10674 | bytes 5869 | solution.py:30
  624.0 25.4 %while.667 = (s32[]{:T(128)}, f32[16,16]{1,0:T(8,128)S(1)}, f32[16,16]{1,0:T(8,128)S(1)}, s32[]{:T(128)}, s32[]{:T(128)}) while((s32[]{:T(128)}, f32[16,16]{1,0:T(8,128)S(1)}, f32[16,16]{1,0:T(8,128)S(1)}, s32[]{:T(128)}, s32[]{:T(128)}) %tuple.1809), condition=%wide.region_18.19_spmd.clone.clone, body=%wide.region_16.18_spmd.clone.clone.sunk | while | flops 7362 | bytes 4572 | solution.py:45
  650.1 28.8 %while.668 = (s32[]{:T(128)}, f32[16,16]{1,0:T(8,128)S(1)}, f32[16,16]{1,0:T(8,128)S(1)}, s32[]{:T(128)}, s32[]{:T(128)}) while((s32[]{:T(128)}, f32[16,16]{1,0:T(8,128)S(1)}, f32[16,16]{1,0:T(8,128)S(1)}, s32[]{:T(128)}, s32[]{:T(128)}) %tuple.1812), condition=%wide.region_21.22_spmd.clone.clone, body=%wide.region_19.21_spmd.clone.clone.sunk | while | flops 10674 | bytes 5869 | solution.py:30
  678.9 25.4 %while.669 = (s32[]{:T(128)}, f32[16,16]{1,0:T(8,128)S(1)}, f32[16,16]{1,0:T(8,128)S(1)}, s32[]{:T(128)}, s32[]{:T(128)}) while((s32[]{:T(128)}, f32[16,16]{1,0:T(8,128)S(1)}, f32[16,16]{1,0:T(8,128)S(1)}, s32[]{:T(128)}, s32[]{:T(128)}) %tuple.1815), condition=%wide.region_24.25_spmd.clone.clone, body=%wide.region_22.24_spmd.clone.clone.sunk | while | flops 7362 | bytes 4572 | solution.py:45
  705.0 28.8 %while.670 = (s32[]{:T(128)}, f32[16,16]{1,0:T(8,128)S(1)}, f32[16,16]{1,0:T(8,128)S(1)}, s32[]{:T(128)}, s32[]{:T(128)}) while((s32[]{:T(128)}, f32[16,16]{1,0:T(8,128)S(1)}, f32[16,16]{1,0:T(8,128)S(1)}, s32[]{:T(128)}, s32[]{:T(128)}) %tuple.1818), condition=%wide.region_27.28_spmd.clone.clone, body=%wide.region_25.27_spmd.clone.clone.sunk | while | flops 10674 | bytes 5869 | solution.py:30
  733.8 25.4 %while.671 = (s32[]{:T(128)}, f32[16,16]{1,0:T(8,128)S(1)}, f32[16,16]{1,0:T(8,128)S(1)}, s32[]{:T(128)}, s32[]{:T(128)}) while((s32[]{:T(128)}, f32[16,16]{1,0:T(8,128)S(1)}, f32[16,16]{1,0:T(8,128)S(1)}, s32[]{:T(128)}, s32[]{:T(128)}) %tuple.1821), condition=%wide.region_30.31_spmd.clone.clone, body=%wide.region_28.30_spmd.clone.clone.sunk | while | flops 7362 | bytes 4572 | solution.py:45
  759.9 28.8 %while.672 = (s32[]{:T(128)}, f32[16,16]{1,0:T(8,128)S(1)}, f32[16,16]{1,0:T(8,128)S(1)}, s32[]{:T(128)}, s32[]{:T(128)}) while((s32[]{:T(128)}, f32[16,16]{1,0:T(8,128)S(1)}, f32[16,16]{1,0:T(8,128)S(1)}, s32[]{:T(128)}, s32[]{:T(128)}) %tuple.1824), condition=%wide.region_33.34_spmd.clone.clone, body=%wide.region_31.33_spmd.clone.clone.sunk | while | flops 10674 | bytes 5869 | solution.py:30
  788.7 25.4 %while.673 = (s32[]{:T(128)}, f32[16,16]{1,0:T(8,128)S(1)}, f32[16,16]{1,0:T(8,128)S(1)}, s32[]{:T(128)}, s32[]{:T(128)}) while((s32[]{:T(128)}, f32[16,16]{1,0:T(8,128)S(1)}, f32[16,16]{1,0:T(8,128)S(1)}, s32[]{:T(128)}, s32[]{:T(128)}) %tuple.1827), condition=%wide.region_36.37_spmd.clone.clone, body=%wide.region_34.36_spmd.clone.clone.sunk | while | flops 7362 | bytes 4572 | solution.py:45
  814.7 28.8 %while.674 = (s32[]{:T(128)}, f32[16,16]{1,0:T(8,128)S(1)}, f32[16,16]{1,0:T(8,128)S(1)}, s32[]{:T(128)}, s32[]{:T(128)}) while((s32[]{:T(128)}, f32[16,16]{1,0:T(8,128)S(1)}, f32[16,16]{1,0:T(8,128)S(1)}, s32[]{:T(128)}, s32[]{:T(128)}) %tuple.1830), condition=%wide.region_39.40_spmd.clone.clone, body=%wide.region_37.39_spmd.clone.clone.sunk | while | flops 10674 | bytes 5869 | solution.py:30
  869.6 28.8 %while.676 = (s32[]{:T(128)}, f32[16,16]{1,0:T(8,128)S(1)}, f32[16,16]{1,0:T(8,128)S(1)}, s32[]{:T(128)}, s32[]{:T(128)}) while((s32[]{:T(128)}, f32[16,16]{1,0:T(8,128)S(1)}, f32[16,16]{1,0:T(8,128)S(1)}, s32[]{:T(128)}, s32[]{:T(128)}) %tuple.1836), condition=%wide.region_45.46_spmd.clone.clone, body=%wide.region_43.45_spmd.clone.clone.sunk | while | flops 10674 | bytes 5869 | solution.py:30
  937.7 28.8 %while.678 = (s32[]{:T(128)}, f32[16,16]{1,0:T(8,128)S(1)}, f32[16,16]{1,0:T(8,128)S(1)}, s32[]{:T(128)}, s32[]{:T(128)}) while((s32[]{:T(128)}, f32[16,16]{1,0:T(8,128)S(1)}, f32[16,16]{1,0:T(8,128)S(1)}, s32[]{:T(128)}, s32[]{:T(128)}) %tuple.1842), condition=%wide.region_51.52_spmd.clone.clone, body=%wide.region_49.51_spmd.clone.clone.sunk | while | flops 10674 | bytes 5869 | solution.py:30
  966.5 25.4 %while.679 = (s32[]{:T(128)}, f32[16,16]{1,0:T(8,128)S(1)}, f32[16,16]{1,0:T(8,128)S(1)}, s32[]{:T(128)}, s32[]{:T(128)}) while((s32[]{:T(128)}, f32[16,16]{1,0:T(8,128)S(1)}, f32[16,16]{1,0:T(8,128)S(1)}, s32[]{:T(128)}, s32[]{:T(128)}) %tuple.1845), condition=%wide.region_54.55_spmd.clone.clone, body=%wide.region_52.54_spmd.clone.clone.sunk | while | flops 7362 | bytes 4572 | solution.py:45
  992.4 28.8 %while.680 = (s32[]{:T(128)}, f32[16,16]{1,0:T(8,128)S(1)}, f32[16,16]{1,0:T(8,128)S(1)}, s32[]{:T(128)}, s32[]{:T(128)}) while((s32[]{:T(128)}, f32[16,16]{1,0:T(8,128)S(1)}, f32[16,16]{1,0:T(8,128)S(1)}, s32[]{:T(128)}, s32[]{:T(128)}) %tuple.1848), condition=%wide.region_57.58_spmd.clone.clone, body=%wide.region_55.57_spmd.clone.clone.sunk | while | flops 10674 | bytes 5869 | solution.py:30
  1021.2 25.4 %while.681 = (s32[]{:T(128)}, f32[16,16]{1,0:T(8,128)S(1)}, f32[16,16]{1,0:T(8,128)S(1)}, s32[]{:T(128)}, s32[]{:T(128)}) while((s32[]{:T(128)}, f32[16,16]{1,0:T(8,128)S(1)}, f32[16,16]{1,0:T(8,128)S(1)}, s32[]{:T(128)}, s32[]{:T(128)}) %tuple.1851), condition=%wide.region_60.61_spmd.clone.clone, body=%wide.region_58.60_spmd.clone.clone.sunk | while | flops 7362 | bytes 4572 | solution.py:45
  1047.1 28.8 %while.682 = (s32[]{:T(128)}, f32[16,16]{1,0:T(8,128)S(1)}, f32[16,16]{1,0:T(8,128)S(1)}, s32[]{:T(128)}, s32[]{:T(128)}) while((s32[]{:T(128)}, f32[16,16]{1,0:T(8,128)S(1)}, f32[16,16]{1,0:T(8,128)S(1)}, s32[]{:T(128)}, s32[]{:T(128)}) %tuple.1854), condition=%wide.region_63.64_spmd.clone.clone, body=%wide.region_61.63_spmd.clone.clone.sunk | while | flops 10674 | bytes 5869 | solution.py:30
  1075.9 25.4 %while.683 = (s32[]{:T(128)}, f32[16,16]{1,0:T(8,128)S(1)}, f32[16,16]{1,0:T(8,128)S(1)}, s32[]{:T(128)}, s32[]{:T(128)}) while((s32[]{:T(128)}, f32[16,16]{1,0:T(8,128)S(1)}, f32[16,16]{1,0:T(8,128)S(1)}, s32[]{:T(128)}, s32[]{:T(128)}) %tuple.1857), condition=%wide.region_66.67_spmd.clone.clone, body=%wide.region_64.66_spmd.clone.clone.sunk | while | flops 7362 | bytes 4572 | solution.py:45
  1101.7 28.8 %while.684 = (s32[]{:T(128)}, f32[16,16]{1,0:T(8,128)S(1)}, f32[16,16]{1,0:T(8,128)S(1)}, s32[]{:T(128)}, s32[]{:T(128)}) while((s32[]{:T(128)}, f32[16,16]{1,0:T(8,128)S(1)}, f32[16,16]{1,0:T(8,128)S(1)}, s32[]{:T(128)}, s32[]{:T(128)}) %tuple.1860), condition=%wide.region_69.70_spmd.clone.clone, body=%wide.region_67.69_spmd.clone.clone.sunk | while | flops 10674 | bytes 5869 | solution.py:30
  1130.5 25.7 %while.685 = (s32[]{:T(128)}, f32[16,16]{1,0:T(8,128)S(1)}, f32[16,16]{1,0:T(8,128)S(1)}, s32[]{:T(128)}, s32[]{:T(128)}) while((s32[]{:T(128)}, f32[16,16]{1,0:T(8,128)S(1)}, f32[16,16]{1,0:T(8,128)S(1)}, s32[]{:T(128)}, s32[]{:T(128)}) %tuple.1863), condition=%wide.region_72.73_spmd.clone.clone, body=%wide.region_70.72_spmd.clone.clone.sunk | while | flops 7362 | bytes 4572 | solution.py:45
  1156.7 28.8 %while.686 = (s32[]{:T(128)}, f32[16,16]{1,0:T(8,128)S(1)}, f32[16,16]{1,0:T(8,128)S(1)}, s32[]{:T(128)}, s32[]{:T(128)}) while((s32[]{:T(128)}, f32[16,16]{1,0:T(8,128)S(1)}, f32[16,16]{1,0:T(8,128)S(1)}, s32[]{:T(128)}, s32[]{:T(128)}) %tuple.1866), condition=%wide.region_75.76_spmd.clone.clone, body=%wide.region_73.75_spmd.clone.clone.sunk | while | flops 10674 | bytes 5869 | solution.py:30
  1185.4 25.4 %while.687 = (s32[]{:T(128)}, f32[16,16]{1,0:T(8,128)S(1)}, f32[16,16]{1,0:T(8,128)S(1)}, s32[]{:T(128)}, s32[]{:T(128)}) while((s32[]{:T(128)}, f32[16,16]{1,0:T(8,128)S(1)}, f32[16,16]{1,0:T(8,128)S(1)}, s32[]{:T(128)}, s32[]{:T(128)}) %tuple.1869), condition=%wide.region_78.79_spmd.clone.clone, body=%wide.region_76.78_spmd.clone.clone.sunk | while | flops 7362 | bytes 4572 | solution.py:45
  1211.3 28.8 %while.688 = (s32[]{:T(128)}, f32[16,16]{1,0:T(8,128)S(1)}, f32[16,16]{1,0:T(8,128)S(1)}, s32[]{:T(128)}, s32[]{:T(128)}) while((s32[]{:T(128)}, f32[16,16]{1,0:T(8,128)S(1)}, f32[16,16]{1,0:T(8,128)S(1)}, s32[]{:T(128)}, s32[]{:T(128)}) %tuple.1872), condition=%wide.region_81.82_spmd.clone.clone, body=%wide.region_79.81_spmd.clone.clone.sunk | while | flops 10674 | bytes 5869 | solution.py:30
  1240.0 25.4 %while.689 = (s32[]{:T(128)}, f32[16,16]{1,0:T(8,128)S(1)}, f32[16,16]{1,0:T(8,128)S(1)}, s32[]{:T(128)}, s32[]{:T(128)}) while((s32[]{:T(128)}, f32[16,16]{1,0:T(8,128)S(1)}, f32[16,16]{1,0:T(8,128)S(1)}, s32[]{:T(128)}, s32[]{:T(128)}) %tuple.1875), condition=%wide.region_84.85_spmd.clone.clone, body=%wide.region_82.84_spmd.clone.clone.sunk | while | flops 7362 | bytes 4572 | solution.py:45
  1265.8 28.8 %while.690 = (s32[]{:T(128)}, f32[16,16]{1,0:T(8,128)S(1)}, f32[16,16]{1,0:T(8,128)S(1)}, s32[]{:T(128)}, s32[]{:T(128)}) while((s32[]{:T(128)}, f32[16,16]{1,0:T(8,128)S(1)}, f32[16,16]{1,0:T(8,128)S(1)}, s32[]{:T(128)}, s32[]{:T(128)}) %tuple.1878), condition=%wide.region_87.88_spmd.clone.clone, body=%wide.region_85.87_spmd.clone.clone.sunk | while | flops 10674 | bytes 5869 | solution.py:30
  1294.6 25.4 %while.691 = (s32[]{:T(128)}, f32[16,16]{1,0:T(8,128)S(1)}, f32[16,16]{1,0:T(8,128)S(1)}, s32[]{:T(128)}, s32[]{:T(128)}) while((s32[]{:T(128)}, f32[16,16]{1,0:T(8,128)S(1)}, f32[16,16]{1,0:T(8,128)S(1)}, s32[]{:T(128)}, s32[]{:T(128)}) %tuple.1881), condition=%wide.region_90.91_spmd.clone.clone, body=%wide.region_88.90_spmd.clone.clone.sunk | while | flops 7362 | bytes 4572 | solution.py:45
  1320.9 28.8 %while.692 = (s32[]{:T(128)}, f32[16,16]{1,0:T(8,128)S(1)}, f32[16,16]{1,0:T(8,128)S(1)}, s32[]{:T(128)}, s32[]{:T(128)}) while((s32[]{:T(128)}, f32[16,16]{1,0:T(8,128)S(1)}, f32[16,16]{1,0:T(8,128)S(1)}, s32[]{:T(128)}, s32[]{:T(128)}) %tuple.1884), condition=%wide.region_93.94_spmd.clone.clone, body=%wide.region_91.93_spmd.clone.clone.sunk | while | flops 10674 | bytes 5869 | solution.py:30
  1524.9 25.4 %while.693 = (s32[]{:T(128)}, f32[16,16]{1,0:T(8,128)S(1)}, f32[16,16]{1,0:T(8,128)S(1)}, s32[]{:T(128)}, s32[]{:T(128)}) while((s32[]{:T(128)}, f32[16,16]{1,0:T(8,128)S(1)}, f32[16,16]{1,0:T(8,128)S(1)}, s32[]{:T(128)}, s32[]{:T(128)}) %tuple.1887), condition=%wide.region_96.97_spmd.clone.clone, body=%wide.region_94.96_spmd.clone.clone.sunk | while | flops 7362 | bytes 4572 | solution.py:45
  1585.0 445.5 %all-reduce.7.cloned.1.call-done = f32[64,256]{1,0:T(8,128)} async-done(((f32[64,256]{1,0:T(8,128)}), f32[64,256]{1,0:T(8,128)}) %all-reduce.7.cloned.1.call-update) | async-done | bytes 65552 | tf_op jit(solution)/shard_map/psum | solution.py:10
  (3201 shorter events, 970.3 us)
Async XLA Ops:
  7.2 0.7 copy-start.5
  7.2 476.4 %all-reduce.5.cloned.1.call-start = ((), (), s32[]{:S(2)}) async-start(), calls=%async_computation | async-start | bytes 524288 | tf_op jit(solution)/shard_map/psum | solution.py:10
  11.0 2019.5 %all-reduce.7.cloned.1.call-start = ((), (), s32[]{:S(2)}) async-start(), calls=%async_computation.1 | async-start | bytes 131072 | tf_op jit(solution)/shard_map/psum | solution.py:10
  484.3 55.4 %copy-start.3 = (f32[256,256]{1,0:T(8,128)S(1)}, f32[256,256]{1,0:T(8,128)}, u32[]{:S(2)}) copy-start(f32[256,256]{1,0:T(8,128)} %all-reduce.5.cloned.1.call-done) | copy-start | bytes 786436
  1362.7 160.9 %copy-start = (f32[256,256]{0,1:T(8,128)}, f32[256,256]{0,1:T(8,128)S(1)}, u32[]{:S(2)}) copy-start(f32[256,256]{0,1:T(8,128)S(1)} %scatter.610) | copy-start | bytes 786436
  1567.2 15.8 copy-start.1
  1583.1 0.9 copy-start.4
  1584.0 448.0 %copy-start.2 = (f32[512,256]{1,0:T(8,128)}, f32[512,256]{1,0:T(8,128)S(1)}, u32[]{:S(2)}) copy-start(f32[512,256]{1,0:T(8,128)S(1)} %fusion.560) | copy-start | bytes 1572868
Sparse Core Ops, SparseCore 0:
  14.0 469.5 all-reduce.4
  1585.1 445.3 all-reduce.6
where the time goes:
time: 2050 us; the launch traced here: 2040 us
  waiting for transfers between devices  918 us (45%)
  matrix products  726 us (35%)
  loops' own time  185 us (9%)
  local copies, waits for them, and re-layouts  151 us (7%)
  other arithmetic  41.9 us (2%)
    psum x2, waiting for transfers between devices, reduce_all(): return lax.psum((terms[0],), ('cells', 'sub'))  918 us
    dot_general x1535, matrix products, matmul(): jnp.dot(left, right, precision=HIGHEST, preferred_element_type=jnp.float32)  717 us
    another operation x16, loops' own time, small_cholesky(): lax.fori_loop(0, width, column_step, jnp.zeros((width, width), jnp.float32))  182 us
    scatter x120, local copies, waits for them, and re-layouts, factorize(): lower_inverse.at[start:finish, begin:begin + block]  99.4 us
  transfers between devices with their start and end apart: 2, of which 2 were waited for; matrix products, arithmetic and copies ran while one was open for 0% of the time, Pallas kernels for 0%

commit v1 on v0

v1 whole, which is shorter than its diff:
```python
import jax
import jax.numpy as jnp
from jax import lax
from jax.experimental import pallas as pl
from jax.experimental.pallas import tpu as pltpu
from jax.sharding import PartitionSpec as P

HIGHEST = lax.Precision.HIGHEST
MESH = pl.DeviceIdType.MESH
F32 = jnp.float32

ORDER = 256
HALF = 128
TILE = 8
TILES = ORDER // TILE
XS = 4
SUBS = 8
PLANE = XS * SUBS
DEPTH = 16


def row_scale(volumes_ref, live_ref):
    rows = volumes_ref.shape[1]
    slots = lax.broadcasted_iota(jnp.int32, (1, rows), 1)
    return jnp.where(slots < live_ref[0], jnp.sqrt(volumes_ref[...]), 0.0)


def column_scale(scale):
    rows = scale.shape[1]
    return jnp.transpose(jnp.broadcast_to(scale, (HALF, rows)))


def scaled_rows(snap_ref, columns, weighted_ref):
    for half in range(2):
        part = slice(HALF * half, HALF * half + HALF)
        weighted_ref[:, part] = snap_ref[:, part] * columns


def reduce_kernel(
    total_rows,
    snap_ref,
    vol_ref,
    live_ref,
    probe_ref,
    out_ref,
    weighted,
    local,
    plane_buf,
    depth_buf,
    full,
    plane_send,
    plane_recv,
    depth_send,
    depth_recv,
    full_send,
    full_recv,
):
    cells = lax.axis_index("cells")
    sub = lax.axis_index("sub")
    z = cells // XS
    x = cells % XS
    me = x * SUBS + sub

    def plane_id(place):
        return (z * XS + place // SUBS, place % SUBS)

    def depth_id(place):
        return (place * XS + x, sub)

    barrier = pltpu.get_barrier_semaphore()

    def greet_depth(step, carry):
        other = (z + DEPTH // 2 + step) % DEPTH

        @pl.when(other != z)
        def _():
            pl.semaphore_signal(
                barrier, inc=1, device_id=depth_id(other), device_id_type=MESH
            )

        return carry

    def greet_plane(step, carry):
        other = (me + step) % PLANE
        pl.semaphore_signal(
            barrier, inc=1, device_id=plane_id(other), device_id_type=MESH
        )
        return carry

    lax.fori_loop(0, DEPTH, greet_depth, 0)
    lax.fori_loop(1, PLANE, greet_plane, 0)

    scale = row_scale(vol_ref, live_ref)
    scaled_rows(snap_ref, column_scale(scale), weighted)
    probe_weighted = probe_ref[...] * scale

    def gram(left, right):
        return lax.dot_general(
            left,
            right,
            (((0,), (0,)), ((), ())),
            precision=HIGHEST,
            preferred_element_type=F32,
        ) * F32(1.0 / total_rows)

    local[0:HALF, :] = gram(weighted[:, 0:HALF], weighted[...])
    local[HALF:ORDER, HALF:ORDER] = gram(
        weighted[:, HALF:ORDER], weighted[:, HALF:ORDER]
    )
    cross = jnp.dot(
        probe_weighted, weighted[...], precision=HIGHEST, preferred_element_type=F32
    )
    count = cross.shape[0]
    local[HALF : HALF + count, 0:HALF] = cross[:, 0:HALF]
    local[HALF + count : HALF + 2 * count, 0:HALF] = cross[:, HALF:ORDER]

    pl.semaphore_wait(barrier, PLANE - 1 + DEPTH - 1)

    def plane_copy(other, mine):
        return pltpu.make_async_remote_copy(
            src_ref=local.at[pl.ds(pl.multiple_of(other * TILE, TILE), TILE), :],
            dst_ref=plane_buf.at[mine],
            send_sem=plane_send.at[other],
            recv_sem=plane_recv.at[mine],
            device_id=plane_id(other),
            device_id_type=MESH,
        )

    def start_plane(step, carry):
        plane_copy((me + step) % PLANE, me).start()
        return carry

    lax.fori_loop(1, PLANE, start_plane, 0)
    total = local[pl.ds(pl.multiple_of(me * TILE, TILE), TILE), :]

    def take_plane(step, total):
        other = (me + PLANE - step) % PLANE
        pltpu.make_async_copy(
            plane_buf.at[other], plane_buf.at[other], plane_recv.at[other]
        ).wait()
        return total + plane_buf[other]

    total = lax.fori_loop(1, PLANE, take_plane, total)

    depth_buf[z] = total

    def depth_copy(other):
        return pltpu.make_async_remote_copy(
            src_ref=depth_buf.at[z],
            dst_ref=depth_buf.at[z],
            send_sem=depth_send.at[other],
            recv_sem=depth_recv.at[z],
            device_id=depth_id(other),
            device_id_type=MESH,
        )

    def start_depth(step, carry):
        far = DEPTH // 2
        depth_copy((z + DEPTH + far - (step + 1) // 2 * (1 - step % 2 * 2)) % DEPTH).start()
        return carry

    lax.fori_loop(0, DEPTH - 1, start_depth, 0)

    def wait_depth(step, carry):
        other = (z + step) % DEPTH
        pltpu.make_async_copy(
            depth_buf.at[other], depth_buf.at[other], depth_recv.at[other]
        ).wait()
        return carry

    lax.fori_loop(1, DEPTH, wait_depth, 0)
    summed = depth_buf[0]
    for place in range(1, DEPTH):
        summed = summed + depth_buf[place]

    mine = pl.ds(pl.multiple_of(me * TILE, TILE), TILE)
    full[mine, :] = summed

    def full_copy(other):
        return pltpu.make_async_remote_copy(
            src_ref=full.at[mine, :],
            dst_ref=full.at[mine, :],
            send_sem=full_send.at[other],
            recv_sem=full_recv.at[me],
            device_id=plane_id(other),
            device_id_type=MESH,
        )

    def start_full(step, carry):
        full_copy((me + step) % PLANE).start()
        return carry

    lax.fori_loop(1, PLANE, start_full, 0)

    def wait_full(step, carry):
        other = (me + PLANE - step) % PLANE
        tile = full.at[pl.ds(pl.multiple_of(other * TILE, TILE), TILE), :]
        pltpu.make_async_copy(tile, tile, full_recv.at[other]).wait()
        return carry

    lax.fori_loop(1, PLANE, wait_full, 0)

    def drain_plane(step, carry):
        other = (me + step) % PLANE
        plane_copy(other, me).wait_send()
        full_copy(other).wait_send()
        return carry

    lax.fori_loop(1, PLANE, drain_plane, 0)

    def drain_depth(step, carry):
        depth_copy((z + step) % DEPTH).wait_send()
        return carry

    lax.fori_loop(1, DEPTH, drain_depth, 0)
    out_ref[...] = full[...]


def lane_spread(block, lane):
    return jnp.broadcast_to(block[:, lane : lane + 1], (TILE, HALF))


def row_spread(block, row):
    return jnp.broadcast_to(block[row : row + 1, :], (TILE, HALF))


def eliminate(work, upper, lower_inverse):
    lane = lax.broadcasted_iota(jnp.int32, (TILE, HALF), 1)
    row_in = lax.broadcasted_iota(jnp.int32, (TILE, HALF), 0)
    diag = [lane_spread(work[0:TILE, 0:HALF], j) for j in range(TILE)]
    for t in range(TILES):
        half, low = divmod(TILE * t, HALF)
        rows_t = slice(TILE * t, TILE * t + TILE)
        current = [work[rows_t, 0:HALF], work[rows_t, HALF:ORDER]]
        unit = jnp.where(lane == low + row_in, 1.0, 0.0)
        inside = (lane >= low) & (lane < low + TILE)
        last = t == TILES - 1
        if not last:
            rows_n = slice(TILE * t + TILE, TILE * t + 2 * TILE)
            after = [work[rows_n, 0:HALF], work[rows_n, HALF:ORDER]]
            half_n, low_n = divmod(TILE * t + TILE, HALF)
            diag_n = [lane_spread(after[half_n], low_n + j) for j in range(TILE)]
            below = [lane_spread(after[half], low + j) for j in range(TILE)]
        pivots, unit_pivots, factors = [], [], []
        for k in range(TILE):
            root = lax.rsqrt(row_spread(diag[k], k))
            column = diag[k] * root
            masked = jnp.where(row_in > k, column, 0.0)
            entries = {j: row_spread(column, j) for j in range(k + 1, TILE)}
            for j in range(k + 1, TILE):
                diag[j] = diag[j] - column * entries[j]
            pivot = [row_spread(current[i], k) * root for i in range(2)]
            unit_pivot = row_spread(unit, k) * root
            if k < TILE - 1:
                current = [current[i] - masked * pivot[i] for i in range(2)]
                unit = unit - masked * unit_pivot
            pivots.append(pivot)
            unit_pivots.append(unit_pivot)
            if not last:
                factor = below[k] * root
                for j in range(k + 1, TILE):
                    below[j] = below[j] - factor * entries[j]
                for j in range(TILE):
                    diag_n[j] = diag_n[j] - factor * row_spread(factor, j)
                factors.append(factor)
        done = list(pivots[0])
        unit_done = unit_pivots[0]
        for k in range(1, TILE):
            done = [jnp.where(row_in == k, pivots[k][i], done[i]) for i in range(2)]
            unit_done = jnp.where(row_in == k, unit_pivots[k], unit_done)
        for i in range(2):
            columns = slice(HALF * i, HALF * i + HALF)
            place = lane + HALF * i
            upper[rows_t, columns] = jnp.where(place >= TILE * t + row_in, done[i], 0.0)
            left = jnp.where(place < TILE * t, done[i], 0.0)
            if i == half:
                left = jnp.where(inside, unit_done, left)
            lower_inverse[rows_t, columns] = left
        if last:
            break
        for k in range(TILE):
            pivots[k][half] = jnp.where(inside, unit_pivots[k], pivots[k][half])
        after[half] = jnp.where(inside, 0.0, after[half])
        for k in range(TILE):
            after = [after[i] - factors[k] * pivots[k][i] for i in range(2)]
        work[rows_n, 0:HALF] = after[0]
        work[rows_n, HALF:ORDER] = after[1]
        diag = diag_n
        if t < TILES - 2:
            turned = {
                i: jnp.transpose(done[i]) for i in range((TILE * t + 2 * TILE) // HALF, 2)
            }
            for s in range(t + 2, TILES):
                rows_s = slice(TILE * s, TILE * s + TILE)
                i_s, low_s = divmod(TILE * s, HALF)
                multipliers = turned[i_s][low_s : low_s + TILE, :]
                tile = [work[rows_s, 0:HALF], work[rows_s, HALF:ORDER]]
                tile[half] = jnp.where(inside, 0.0, tile[half])
                for k in range(TILE):
                    spread = lane_spread(multipliers, k)
                    tile = [tile[i] - spread * pivots[k][i] for i in range(2)]
                work[rows_s, 0:HALF] = tile[0]
                work[rows_s, HALF:ORDER] = tile[1]


def finish_kernel(
    root_total,
    sums_ref,
    snap_ref,
    vol_ref,
    live_ref,
    basis_ref,
    factor_ref,
    coef_ref,
    work,
    inverse,
    weighted,
):
    count = coef_ref.shape[0]
    work[0:HALF, :] = sums_ref[0:HALF, :]
    work[HALF:ORDER, HALF:ORDER] = sums_ref[HALF:ORDER, HALF:ORDER]
    work[HALF:ORDER, 0:HALF] = jnp.transpose(sums_ref[0:HALF, HALF:ORDER])
    scale = row_scale(vol_ref, live_ref)
    scaled_rows(snap_ref, column_scale(scale), weighted)
    eliminate(work, factor_ref, inverse)

    def apply(left):
        return lax.dot_general(
            left,
            inverse[...],
            (((1,), (1,)), ((), ())),
            precision=HIGHEST,
            preferred_element_type=F32,
        )

    basis_ref[...] = apply(weighted[...])
    cross = jnp.concatenate(
        [
            sums_ref[HALF : HALF + count, 0:HALF],
            sums_ref[HALF + count : HALF + 2 * count, 0:HALF],
        ],
        axis=1,
    )
    coef_ref[...] = apply(cross) / F32(root_total)


def per_device(snapshots, volumes, live_rows, probes):
    row_count = snapshots.shape[0]
    total_rows = row_count * PLANE * DEPTH
    in_vmem = pl.BlockSpec(memory_space=pltpu.VMEM)
    in_smem = pl.BlockSpec(memory_space=pltpu.SMEM)
    volumes = volumes.reshape(1, row_count)
    dma = pltpu.SemaphoreType.DMA

    def reduce_body(*refs):
        reduce_kernel(total_rows, *refs)

    sums = pl.pallas_call(
        reduce_body,
        out_shape=jax.ShapeDtypeStruct((ORDER, ORDER), F32),
        in_specs=[in_vmem, in_vmem, in_smem, in_vmem],
        out_specs=in_vmem,
        scratch_shapes=[
            pltpu.VMEM((row_count, ORDER), F32),
            pltpu.VMEM((ORDER, ORDER), F32),
            pltpu.VMEM((PLANE, TILE, ORDER), F32),
            pltpu.VMEM((DEPTH, TILE, ORDER), F32),
            pltpu.VMEM((ORDER, ORDER), F32),
            dma((PLANE,)),
            dma((PLANE,)),
            dma((DEPTH,)),
            dma((DEPTH,)),
            dma((PLANE,)),
            dma((PLANE,)),
        ],
        compiler_params=pltpu.CompilerParams(collective_id=0, has_side_effects=True),
        name="reduce_sums",
    )(snapshots, volumes, live_rows, probes)

    def finish_body(*refs):
        finish_kernel(float(total_rows) ** 0.5, *refs)

    return pl.pallas_call(
        finish_body,
        out_shape=(
            jax.ShapeDtypeStruct((row_count, ORDER), F32),
            jax.ShapeDtypeStruct((ORDER, ORDER), F32),
            jax.ShapeDtypeStruct((probes.shape[0], ORDER), F32),
        ),
        in_specs=[in_vmem, in_vmem, in_vmem, in_smem],
        out_specs=(in_vmem, in_vmem, in_vmem),
        scratch_shapes=[
            pltpu.VMEM((ORDER, ORDER), F32),
            pltpu.VMEM((ORDER, ORDER), F32),
            pltpu.VMEM((row_count, ORDER), F32),
        ],
        name="factor_apply",
    )(sums, snapshots, volumes, live_rows)


def solution(mesh):
    both = ("cells", "sub")
    placed = (P(both, None), P(both), P(both), P(None, both))
    return jax.shard_map(
        per_device,
        mesh=mesh,
        in_specs=placed,
        out_specs=(P(both, None), P(), P()),
        check_vma=False,
    )
```

time: 2050 us -> 58.3 us (0.03)
  waiting for transfers between devices: 918 us -> 0 us
  matrix products: 726 us -> 0 us
  loops' own time: 185 us -> 0 us
  local copies, waits for them, and re-layouts: 151 us -> 0 us
  Pallas kernels: 0 us -> 56.8 us
  other arithmetic: 41.9 us -> 0 us
    psum x2 -> x0, waiting for transfers between devices: 918 us -> none  [reduce_all(): return lax.psum((terms[0],), ('cells', 'sub'))]
    dot_general x1553 -> x0, matrix products: 726 us -> none  [the longest x1535 717 us: matmul(): jnp.dot(left, right, precision=HIGHEST, preferred_element_type=jnp.float32)]
    another operation x32 -> x0, loops' own time: 185 us -> none  [the longest x16 182 us: small_cholesky(): lax.fori_loop(0, width, column_step, jnp.zeros((width, width), jnp.float32))]
    scatter x166 -> x0, local copies, waits for them, and re-layouts: 139 us -> none  [the longest x120 99.4 us: factorize(): lower_inverse.at[start:finish, begin:begin + block]]
    pallas_call x0 -> x2, Pallas kernels: none -> 56.8 us  [the longest x1 41.2 us: per_device(): pl.pallas_call(reduce_body, out_shape=jax.ShapeDtypeStruct((ORDER, ORDER)...]
    add x512 -> x0, other arithmetic: 38.6 us -> none  [the longest x256 19.3 us: row_step(): return result + unit[:, None] * solved[None, :]]
  transfers between devices with their start and end apart: 2 -> 0, of which waited for: 2 -> 0; matrix products, arithmetic and copies ran while one was open for 0% -> 0% of each run, Pallas kernels for 0% -> 0%
where the time goes in v1:
time: 58.3 us; the launch traced here: 58.1 us
  Pallas kernels  56.8 us (97%)
  between operations  1.28 us (2%)
    pallas_call x1, Pallas kernels, per_device(): pl.pallas_call(reduce_body, out_shape=jax.ShapeDtypeStruct((ORDER, ORDER)...  41.2 us
    pallas_call x1, Pallas kernels, per_device(): pl.pallas_call(finish_body, out_shape=(jax.ShapeDtypeStruct((row_count, O...  15.6 us

profile of v1, /device:TPU:1, one launch (start us, length us, event | category | flops | bytes accessed | tf_op | source)
XLA Modules:
  0.0 58.1 jit_solution(1694496966413417888)
XLA Ops:
  1.3 41.2 %reduce_sums.1.refs_0_ = f32[256,256]{1,0:T(8,128)} custom-call(f32[512,256]{1,0:T(8,128)} %refs_1_.1, f32[1,512]{1,0:T(1,128)} %bitcast.1, s32[1]{0:T(128)S(6)} %copy.7.refs_2_.refs_3_, f32[64,512]{1,0:T(8,128)} %refs_3_.2), custom_call_target="tpu_custom_call" | custom-call | tf_op jit(solution)/shard_map/reduce_sums/pallas_call | solution.py:358
  42.5 15.6 %factor_apply.1 = (f32[512,256]{1,0:T(8,128)}, f32[256,256]{1,0:T(8,128)}, f32[64,256]{1,0:T(8,128)}) custom-call(f32[256,256]{1,0:T(8,128)} %reduce_sums.1.refs_0_, f32[512,256]{1,0:T(8,128)} %refs_1_.1, f32[1,512]{1,0:T(1,128)} %bitcast.2, s32[1]{0:T(128)S(6)} %copy.7.refs_2_.refs_3_), custom_call_target="tpu_custom_call" | custom-call | tf_op jit(solution)/shard_map/factor_apply/pallas_call | solution.py:383

commit v2 on v1

v2 whole, which is shorter than its diff:
```python
import jax
import jax.numpy as jnp
from jax import lax
from jax.experimental import pallas as pl
from jax.experimental.pallas import tpu as pltpu
from jax.sharding import PartitionSpec as P

HIGHEST = lax.Precision.HIGHEST
MESH = pl.DeviceIdType.MESH
F32 = jnp.float32

ORDER = 256
HALF = 128
TILE = 8
TILES = ORDER // TILE
PANEL = 8
XS = 4
YS = 4
CORES = 2
PLANE = XS * YS
DEPTH = 16


def reduce_kernel(
    total_rows,
    snap_hbm,
    vol_hbm,
    live_hbm,
    probe_hbm,
    out_ref,
    weighted,
    snap,
    vol,
    live,
    probe,
    local,
    pair_buf,
    plane_buf,
    depth_buf,
    full,
    load_sems,
    pair_sems,
    plane_send,
    plane_recv,
    depth_send,
    depth_recv,
    full_send,
    full_recv,
    cross_send,
    cross_recv,
):
    cells = lax.axis_index("cells")
    sub = lax.axis_index("sub")
    z = cells // XS
    x = cells % XS
    y = sub // CORES
    core = sub % CORES
    me = x * YS + y

    def pair_id():
        return (cells, y * CORES + 1 - core)

    def plane_id(place):
        return (z * XS + place // YS, place % YS * CORES + core)

    def depth_id(place):
        return (place * XS + x, sub)

    loads = [
        pltpu.make_async_copy(source, target, load_sems.at[i])
        for i, (source, target) in enumerate(
            [(live_hbm, live), (vol_hbm, vol), (snap_hbm, snap), (probe_hbm, probe)]
        )
    ]
    for load in loads:
        load.start()

    barrier = pltpu.get_barrier_semaphore()

    def greet_depth(step, carry):
        pl.semaphore_signal(
            barrier,
            inc=1,
            device_id=depth_id((z + DEPTH // 2 + step) % DEPTH),
            device_id_type=MESH,
        )
        return carry

    def greet_plane(step, carry):
        pl.semaphore_signal(
            barrier,
            inc=1,
            device_id=plane_id((me + step) % PLANE),
            device_id_type=MESH,
        )
        return carry

    lax.fori_loop(0, DEPTH // 2, greet_depth, 0)
    lax.fori_loop(DEPTH // 2 + 1, DEPTH, greet_depth, 0)
    lax.fori_loop(1, PLANE, greet_plane, 0)
    pl.semaphore_signal(barrier, inc=1, device_id=pair_id(), device_id_type=MESH)

    loads[0].wait()
    loads[1].wait()
    rows = vol.shape[1]
    slots = lax.broadcasted_iota(jnp.int32, (1, rows), 1)
    scale = jnp.where(slots < live[0], jnp.sqrt(vol[...]), 0.0)
    columns = jnp.transpose(jnp.broadcast_to(scale, (HALF, rows)))
    loads[2].wait()
    for half in range(2):
        part = slice(HALF * half, HALF * half + HALF)
        weighted[:, part] = snap[:, part] * columns

    def gram(left, right):
        return lax.dot_general(
            left,
            right,
            (((0,), (0,)), ((), ())),
            precision=HIGHEST,
            preferred_element_type=F32,
        ) * F32(1.0 / total_rows)

    local[0:HALF, :] = gram(weighted[:, 0:HALF], weighted[...])
    local[HALF:ORDER, HALF:ORDER] = gram(
        weighted[:, HALF:ORDER], weighted[:, HALF:ORDER]
    )
    loads[3].wait()
    cross = jnp.dot(
        probe[...] * scale, weighted[...], precision=HIGHEST, preferred_element_type=F32
    )
    count = cross.shape[0]
    local[HALF : HALF + count, 0:HALF] = cross[:, 0:HALF]
    local[HALF + count : HALF + 2 * count, 0:HALF] = cross[:, HALF:ORDER]

    pl.semaphore_wait(barrier, 1 + PLANE - 1 + DEPTH - 1)

    def half_rows(which):
        return pl.ds(pl.multiple_of(which * HALF, HALF), HALF)

    pair = pltpu.make_async_remote_copy(
        src_ref=local.at[half_rows(1 - core), :],
        dst_ref=pair_buf,
        send_sem=pair_sems.at[0],
        recv_sem=pair_sems.at[1],
        device_id=pair_id(),
        device_id_type=MESH,
    )
    pair.start()
    pair.wait()
    pair_buf[...] = pair_buf[...] + local[half_rows(core), :]

    def tile_of(place):
        return pl.ds(pl.multiple_of(place * TILE, TILE), TILE)

    def plane_copy(other):
        return pltpu.make_async_remote_copy(
            src_ref=pair_buf.at[tile_of(other), :],
            dst_ref=plane_buf.at[me],
            send_sem=plane_send.at[other],
            recv_sem=plane_recv.at[me],
            device_id=plane_id(other),
            device_id_type=MESH,
        )

    def start_plane(step, carry):
        plane_copy((me + step) % PLANE).start()
        return carry

    lax.fori_loop(1, PLANE, start_plane, 0)

    def take_plane(step, total):
        other = (me + PLANE - step) % PLANE
        pltpu.make_async_copy(
            plane_buf.at[other], plane_buf.at[other], plane_recv.at[other]
        ).wait()
        return total + plane_buf[other]

    total = lax.fori_loop(1, PLANE, take_plane, pair_buf[tile_of(me), :])

    depth_buf[z] = total

    def depth_copy(other):
        return pltpu.make_async_remote_copy(
            src_ref=depth_buf.at[z],
            dst_ref=depth_buf.at[z],
            send_sem=depth_send.at[other],
            recv_sem=depth_recv.at[z],
            device_id=depth_id(other),
            device_id_type=MESH,
        )

    def start_depth(step, carry):
        far = DEPTH // 2
        near = (step + 1) // 2 * (1 - step % 2 * 2)
        depth_copy((z + DEPTH + far - near) % DEPTH).start()
        return carry

    lax.fori_loop(0, DEPTH - 1, start_depth, 0)

    def wait_depth(step, carry):
        other = (z + step) % DEPTH
        pltpu.make_async_copy(
            depth_buf.at[other], depth_buf.at[other], depth_recv.at[other]
        ).wait()
        return carry

    lax.fori_loop(1, DEPTH, wait_depth, 0)
    summed = depth_buf[0]
    for place in range(1, DEPTH):
        summed = summed + depth_buf[place]

    def own_tile(place):
        return pl.ds(pl.multiple_of(core * HALF + place * TILE, TILE), TILE)

    full[own_tile(me), :] = summed

    def full_copy(other):
        return pltpu.make_async_remote_copy(
            src_ref=full.at[own_tile(me), :],
            dst_ref=full.at[own_tile(me), :],
            send_sem=full_send.at[other],
            recv_sem=full_recv.at[me],
            device_id=plane_id(other),
            device_id_type=MESH,
        )

    def cross_copy(place):
        return pltpu.make_async_remote_copy(
            src_ref=full.at[own_tile(place), :],
            dst_ref=full.at[own_tile(place), :],
            send_sem=cross_send.at[place],
            recv_sem=cross_recv.at[place],
            device_id=pair_id(),
            device_id_type=MESH,
        )

    def start_full(step, carry):
        full_copy((me + step) % PLANE).start()
        return carry

    lax.fori_loop(1, PLANE, start_full, 0)
    cross_copy(me).start()

    def hand_on(step, carry):
        other = (me + PLANE - step) % PLANE
        tile = full.at[own_tile(other), :]
        pltpu.make_async_copy(tile, tile, full_recv.at[other]).wait()
        cross_copy(other).start()
        return carry

    lax.fori_loop(1, PLANE, hand_on, 0)

    def drain(step, carry):
        other = (me + step) % PLANE
        plane_copy(other).wait_send()
        full_copy(other).wait_send()
        return carry

    lax.fori_loop(1, PLANE, drain, 0)

    def drain_depth(step, carry):
        depth_copy((z + step) % DEPTH).wait_send()
        return carry

    lax.fori_loop(1, DEPTH, drain_depth, 0)

    def wait_cross(place, carry):
        cross_copy(place).wait_send()
        tile = full.at[
            pl.ds(pl.multiple_of((1 - core) * HALF + place * TILE, TILE), TILE), :
        ]
        pltpu.make_async_copy(tile, tile, cross_recv.at[place]).wait()
        return carry

    lax.fori_loop(0, PLANE, wait_cross, 0)
    out_ref[...] = full[...]


def lane_spread(block, lane):
    return jnp.broadcast_to(block[:, lane : lane + 1], (TILE, HALF))


def row_spread(block, row):
    return jnp.broadcast_to(block[row : row + 1, :], (TILE, HALF))


def stack_rows(row_in, rows):
    stacked = rows[0]
    for k in range(1, TILE):
        stacked = jnp.where(row_in == k, rows[k], stacked)
    return stacked


def eliminate(work, upper, lower_inverse, panel_rows):
    lane = lax.broadcasted_iota(jnp.int32, (TILE, HALF), 1)
    row_in = lax.broadcasted_iota(jnp.int32, (TILE, HALF), 0)
    for t in range(TILES):
        end = (t // PANEL + 1) * PANEL
        half, low = divmod(TILE * t, HALF)
        rows_t = slice(TILE * t, TILE * t + TILE)
        current = [work[rows_t, 0:HALF], work[rows_t, HALF:ORDER]]
        if t % PANEL == 0:
            diag = [lane_spread(current[half], low + j) for j in range(TILE)]
        unit = jnp.where(lane == low + row_in, 1.0, 0.0)
        inside = (lane >= low) & (lane < low + TILE)
        last = t == end - 1
        if not last:
            rows_n = slice(TILE * t + TILE, TILE * t + 2 * TILE)
            after = [work[rows_n, 0:HALF], work[rows_n, HALF:ORDER]]
            half_n, low_n = divmod(TILE * t + TILE, HALF)
            diag_n = [lane_spread(after[half_n], low_n + j) for j in range(TILE)]
            below = [lane_spread(after[half], low + j) for j in range(TILE)]
        pivots, unit_pivots, factors = [], [], []
        for k in range(TILE):
            root = lax.rsqrt(row_spread(diag[k], k))
            column = diag[k] * root
            masked = jnp.where(row_in > k, column, 0.0)
            entries = {j: row_spread(column, j) for j in range(k + 1, TILE)}
            for j in range(k + 1, TILE):
                diag[j] = diag[j] - column * entries[j]
            pivot = [row_spread(current[i], k) * root for i in range(2)]
            unit_pivot = row_spread(unit, k) * root
            if k < TILE - 1:
                current = [current[i] - masked * pivot[i] for i in range(2)]
                unit = unit - masked * unit_pivot
            pivots.append(pivot)
            unit_pivots.append(unit_pivot)
            if not last:
                factor = below[k] * root
                for j in range(k + 1, TILE):
                    below[j] = below[j] - factor * entries[j]
                for j in range(TILE):
                    diag_n[j] = diag_n[j] - factor * row_spread(factor, j)
                factors.append(factor)
        own = stack_rows(row_in, [pivots[k][half] for k in range(TILE)])
        for k in range(TILE):
            pivots[k][half] = jnp.where(inside, unit_pivots[k], pivots[k][half])
        done = [
            stack_rows(row_in, [pivots[k][i] for k in range(TILE)]) for i in range(2)
        ]
        for i in range(2):
            columns = slice(HALF * i, HALF * i + HALF)
            place = lane + HALF * i
            lower_inverse[rows_t, columns] = jnp.where(
                place < TILE * t + TILE, done[i], 0.0
            )
            shown = jnp.where(inside, own, done[i]) if i == half else done[i]
            upper[rows_t, columns] = jnp.where(place >= TILE * t + row_in, shown, 0.0)
            panel_rows[TILE * (t % PANEL) : TILE * (t % PANEL) + TILE, columns] = (
                jnp.where(
                    (place >= TILE * t + TILE) & (place < TILE * end), 0.0, done[i]
                )
            )
        if not last:
            after[half] = jnp.where(inside, 0.0, after[half])
            for k in range(TILE):
                after = [after[i] - factors[k] * pivots[k][i] for i in range(2)]
            work[rows_n, 0:HALF] = after[0]
            work[rows_n, HALF:ORDER] = after[1]
            diag = diag_n
            rest = range(t + 2, end)
            if len(rest) > 0:
                halves = range((TILE * t + 2 * TILE) // HALF, (TILE * end - 1) // HALF + 1)
                turned = {i: jnp.transpose(done[i]) for i in halves}
                tiles = {}
                for s in rest:
                    rows_s = slice(TILE * s, TILE * s + TILE)
                    tiles[s] = [work[rows_s, 0:HALF], work[rows_s, HALF:ORDER]]
                    tiles[s][half] = jnp.where(inside, 0.0, tiles[s][half])
                for k in range(TILE):
                    for s in rest:
                        i_s, low_s = divmod(TILE * s, HALF)
                        spread = lane_spread(turned[i_s][low_s : low_s + TILE, :], k)
                        tiles[s] = [
                            tiles[s][i] - spread * pivots[k][i] for i in range(2)
                        ]
                for s in rest:
                    rows_s = slice(TILE * s, TILE * s + TILE)
                    work[rows_s, 0:HALF] = tiles[s][0]
                    work[rows_s, HALF:ORDER] = tiles[s][1]
        elif end < TILES:
            reached = TILE * end
            first = reached - TILE * PANEL
            turned = jnp.transpose(panel_rows[...])
            update = jnp.dot(
                turned[reached:, :],
                panel_rows[...],
                precision=HIGHEST,
                preferred_element_type=F32,
            )
            place = lax.broadcasted_iota(jnp.int32, (ORDER - reached, ORDER), 1)
            in_panel = (place >= first) & (place < reached)
            work[reached:, :] = jnp.where(in_panel, 0.0, work[reached:, :]) - update


def finish_kernel(
    root_total,
    sums_ref,
    weighted,
    basis_hbm,
    factor_hbm,
    coef_hbm,
    work,
    upper,
    inverse,
    panel_rows,
    basis,
    coef,
    sems,
):
    count = coef.shape[0]
    work[0:HALF, :] = sums_ref[0:HALF, :]
    work[HALF:ORDER, HALF:ORDER] = sums_ref[HALF:ORDER, HALF:ORDER]
    work[HALF:ORDER, 0:HALF] = jnp.transpose(sums_ref[0:HALF, HALF:ORDER])
    eliminate(work, upper, inverse, panel_rows)
    copies = [pltpu.make_async_copy(upper, factor_hbm, sems.at[0])]
    copies[0].start()

    def apply(left):
        return lax.dot_general(
            left,
            inverse[...],
            (((1,), (1,)), ((), ())),
            precision=HIGHEST,
            preferred_element_type=F32,
        )

    cross = jnp.concatenate(
        [
            sums_ref[HALF : HALF + count, 0:HALF],
            sums_ref[HALF + count : HALF + 2 * count, 0:HALF],
        ],
        axis=1,
    )
    coef[...] = apply(cross) / F32(root_total)
    copies.append(pltpu.make_async_copy(coef, coef_hbm, sems.at[1]))
    copies[1].start()
    for part in range(basis.shape[0] // HALF):
        rows = slice(HALF * part, HALF * part + HALF)
        basis[rows, :] = apply(weighted[rows, :])
        copies.append(
            pltpu.make_async_copy(
                basis.at[rows, :], basis_hbm.at[rows, :], sems.at[2 + part]
            )
        )
        copies[-1].start()
    for copy in copies:
        copy.wait()


def per_device(snapshots, volumes, live_rows, probes):
    row_count = snapshots.shape[0]
    count = probes.shape[0]
    total_rows = row_count * CORES * PLANE * DEPTH
    in_vmem = pl.BlockSpec(memory_space=pltpu.VMEM)
    anywhere = pl.BlockSpec(memory_space=pl.ANY)
    volumes = volumes.reshape(1, row_count)
    dma = pltpu.SemaphoreType.DMA

    def reduce_body(*refs):
        reduce_kernel(total_rows, *refs)

    sums, weighted = pl.pallas_call(
        reduce_body,
        out_shape=(
            pltpu.VMEM((ORDER, ORDER), F32),
            pltpu.VMEM((row_count, ORDER), F32),
        ),
        in_specs=[pl.BlockSpec(memory_space=pltpu.HBM)] * 4,
        out_specs=(in_vmem, in_vmem),
        scratch_shapes=[
            pltpu.VMEM((row_count, ORDER), F32),
            pltpu.VMEM((1, row_count), F32),
            pltpu.SMEM((1,), jnp.int32),
            pltpu.VMEM((count, row_count), F32),
            pltpu.VMEM((ORDER, ORDER), F32),
            pltpu.VMEM((HALF, ORDER), F32),
            pltpu.VMEM((PLANE, TILE, ORDER), F32),
            pltpu.VMEM((DEPTH, TILE, ORDER), F32),
            pltpu.VMEM((ORDER, ORDER), F32),
            dma((4,)),
            dma((2,)),
            dma((PLANE,)),
            dma((PLANE,)),
            dma((DEPTH,)),
            dma((DEPTH,)),
            dma((PLANE,)),
            dma((PLANE,)),
            dma((PLANE,)),
            dma((PLANE,)),
        ],
        compiler_params=pltpu.CompilerParams(collective_id=0, has_side_effects=True),
        name="reduce_sums",
    )(snapshots, volumes, live_rows, probes)

    def finish_body(*refs):
        finish_kernel(float(total_rows) ** 0.5, *refs)

    return pl.pallas_call(
        finish_body,
        out_shape=(
            jax.ShapeDtypeStruct((row_count, ORDER), F32),
            jax.ShapeDtypeStruct((ORDER, ORDER), F32),
            jax.ShapeDtypeStruct((count, ORDER), F32),
        ),
        in_specs=[in_vmem, in_vmem],
        out_specs=(anywhere, anywhere, anywhere),
        scratch_shapes=[
            pltpu.VMEM((ORDER, ORDER), F32),
            pltpu.VMEM((ORDER, ORDER), F32),
            pltpu.VMEM((ORDER, ORDER), F32),
            pltpu.VMEM((TILE * PANEL, ORDER), F32),
            pltpu.VMEM((row_count, ORDER), F32),
            pltpu.VMEM((count, ORDER), F32),
            dma((2 + row_count // HALF,)),
        ],
        name="factor_apply",
    )(
        pltpu.with_memory_space_constraint(sums, pltpu.VMEM),
        pltpu.with_memory_space_constraint(weighted, pltpu.VMEM),
    )


def solution(mesh):
    both = ("cells", "sub")
    placed = (P(both, None), P(both), P(both), P(None, both))
    return jax.shard_map(
        per_device,
        mesh=mesh,
        in_specs=placed,
        out_specs=(P(both, None), P(), P()),
        check_vma=False,
    )
```

time: 58.3 us -> 50.6 us (0.87)
  Pallas kernels: 56.8 us -> 49.2 us
    pallas_call x1, Pallas kernels: 15.6 us -> 9.82 us  [per_device(): pl.pallas_call(finish_body, out_shape=(jax.ShapeDtypeStruct((row_count, O...]
    pallas_call x1, Pallas kernels: 41.2 us -> 39.4 us  [per_device(): pl.pallas_call(reduce_body, out_shape=(pltpu.VMEM((ORDER, ORDER), F32), p...]
where the time goes in v2:
time: 50.6 us; the launch traced here: 50.5 us
  Pallas kernels  49.2 us (97%)
  between operations  1.28 us (3%)
    pallas_call x1, Pallas kernels, per_device(): pl.pallas_call(reduce_body, out_shape=(pltpu.VMEM((ORDER, ORDER), F32), p...  39.4 us
    pallas_call x1, Pallas kernels, per_device(): pl.pallas_call(finish_body, out_shape=(jax.ShapeDtypeStruct((row_count, O...  9.82 us

profile of v2, /device:TPU:1, one launch (start us, length us, event | category | flops | bytes accessed | tf_op | source)
XLA Modules:
  0.0 50.5 jit_solution(5082792203821952016)
XLA Ops:
  1.3 39.4 %reduce_sums.1 = (f32[256,256]{1,0:T(8,128)S(1)}, f32[512,256]{1,0:T(8,128)S(1)}) custom-call(f32[512,256]{1,0:T(8,128)} %refs_0_.1, f32[1,512]{1,0:T(1,128)} %bitcast.1, s32[1]{0:T(128)S(6)} %copy.7.refs_2_, f32[64,512]{1,0:T(8,128)} %refs_3_.1), custom_call_target="tpu_custom_call" | custom-call | tf_op jit(solution)/shard_map/reduce_sums/pallas_call | solution.py:463
  40.7 9.8 %factor_apply.1 = (f32[512,256]{1,0:T(8,128)}, f32[256,256]{1,0:T(8,128)}, f32[64,256]{1,0:T(8,128)}) custom-call(f32[256,256]{1,0:T(8,128)S(1)} %get-tuple-element.5.refs_0_, f32[512,256]{1,0:T(8,128)S(1)} %get-tuple-element.6.refs_1_), custom_call_target="tpu_custom_call" | custom-call | tf_op jit(solution)/shard_map/factor_apply/pallas_call | solution.py:499

commit v3 on v2

--- a/solution.py
+++ b/solution.py
@@ -19,6 +19,13 @@
 CORES = 2
 PLANE = XS * YS
 DEPTH = 16
+RELAYS = (1, 2, 4)
+
+
+def plane_offsets():
+    places = [(dx, dy) for dx in range(XS) for dy in range(YS)]
+    hops = lambda place: sum(min(d, 4 - d) for d in place)
+    return sorted(places, key=hops, reverse=True)[:-1]
 
 
 def reduce_kernel(
@@ -39,6 +46,7 @@
     depth_buf,
     full,
     load_sems,
+    relay_sems,
     pair_sems,
     plane_send,
     plane_recv,
@@ -66,6 +74,19 @@
     def depth_id(place):
         return (place * XS + x, sub)
 
+    targets = [(x + dx) % XS * YS + (y + dy) % YS for dx, dy in plane_offsets()]
+    sources = [
+        (x + XS - dx) % XS * YS + (y + YS - dy) % YS
+        for dx, dy in reversed(plane_offsets())
+    ]
+
+    def signal(sem, device):
+        pl.semaphore_signal(sem, inc=1, device_id=device, device_id_type=MESH)
+
+    def relay(stage):
+        for step in (RELAYS[stage], DEPTH - RELAYS[stage]):
+            signal(relay_sems.at[stage], depth_id((z + step) % DEPTH))
+
     loads = [
         pltpu.make_async_copy(source, target, load_sems.at[i])
         for i, (source, target) in enumerate(
@@ -76,29 +97,11 @@
         load.start()
 
     barrier = pltpu.get_barrier_semaphore()
-
-    def greet_depth(step, carry):
-        pl.semaphore_signal(
-            barrier,
-            inc=1,
-            device_id=depth_id((z + DEPTH // 2 + step) % DEPTH),
-            device_id_type=MESH,
-        )
-        return carry
-
-    def greet_plane(step, carry):
-        pl.semaphore_signal(
-            barrier,
-            inc=1,
-            device_id=plane_id((me + step) % PLANE),
-            device_id_type=MESH,
-        )
-        return carry
-
-    lax.fori_loop(0, DEPTH // 2, greet_depth, 0)
-    lax.fori_loop(DEPTH // 2 + 1, DEPTH, greet_depth, 0)
-    lax.fori_loop(1, PLANE, greet_plane, 0)
-    pl.semaphore_signal(barrier, inc=1, device_id=pair_id(), device_id_type=MESH)
+    for other in targets:
+        signal(barrier, plane_id(other))
+    for step in (1, DEPTH - 1):
+        signal(barrier, depth_id((z + step) % DEPTH))
+    signal(barrier, pair_id())
 
     loads[0].wait()
     loads[1].wait()
@@ -132,7 +135,8 @@
     local[HALF : HALF + count, 0:HALF] = cross[:, 0:HALF]
     local[HALF + count : HALF + 2 * count, 0:HALF] = cross[:, HALF:ORDER]
 
-    pl.semaphore_wait(barrier, 1 + PLANE - 1 + DEPTH - 1)
+    pl.semaphore_wait(barrier, 1 + PLANE - 1 + 2)
+    relay(0)
 
     def half_rows(which):
         return pl.ds(pl.multiple_of(which * HALF, HALF), HALF)
@@ -146,6 +150,8 @@
         device_id_type=MESH,
     )
     pair.start()
+    pl.semaphore_wait(relay_sems.at[0], 2)
+    relay(1)
     pair.wait()
     pair_buf[...] = pair_buf[...] + local[half_rows(core), :]
 
@@ -162,20 +168,16 @@
             device_id_type=MESH,
         )
 
-    def start_plane(step, carry):
-        plane_copy((me + step) % PLANE).start()
-        return carry
-
-    lax.fori_loop(1, PLANE, start_plane, 0)
-
-    def take_plane(step, total):
-        other = (me + PLANE - step) % PLANE
+    for other in targets:
+        plane_copy(other).start()
+    pl.semaphore_wait(relay_sems.at[1], 2)
+    relay(2)
+    total = pair_buf[tile_of(me), :]
+    for other in sources:
         pltpu.make_async_copy(
             plane_buf.at[other], plane_buf.at[other], plane_recv.at[other]
         ).wait()
-        return total + plane_buf[other]
-
-    total = lax.fori_loop(1, PLANE, take_plane, pair_buf[tile_of(me), :])
+        total = total + plane_buf[other]
 
     depth_buf[z] = total
 
@@ -195,6 +197,7 @@
         depth_copy((z + DEPTH + far - near) % DEPTH).start()
         return carry
 
+    pl.semaphore_wait(relay_sems.at[2], 2)
     lax.fori_loop(0, DEPTH - 1, start_depth, 0)
 
     def wait_depth(step, carry):
@@ -234,21 +237,13 @@
             device_id_type=MESH,
         )
 
-    def start_full(step, carry):
-        full_copy((me + step) % PLANE).start()
-        return carry
-
-    lax.fori_loop(1, PLANE, start_full, 0)
+    for other in targets:
+        full_copy(other).start()
     cross_copy(me).start()
-
-    def hand_on(step, carry):
-        other = (me + PLANE - step) % PLANE
+    for other in sources:
         tile = full.at[own_tile(other), :]
         pltpu.make_async_copy(tile, tile, full_recv.at[other]).wait()
         cross_copy(other).start()
-        return carry
-
-    lax.fori_loop(1, PLANE, hand_on, 0)
 
     def drain(step, carry):
         other = (me + step) % PLANE
@@ -479,6 +474,7 @@
             pltpu.VMEM((DEPTH, TILE, ORDER), F32),
             pltpu.VMEM((ORDER, ORDER), F32),
             dma((4,)),
+            pltpu.SemaphoreType.REGULAR((len(RELAYS),)),
             dma((2,)),
             dma((PLANE,)),
             dma((PLANE,)),

time: 50.6 us -> 48.9 us (0.966)
  Pallas kernels: 49.2 us -> 47.5 us
    pallas_call x1, Pallas kernels: 39.4 us -> 37.6 us  [per_device(): pl.pallas_call(reduce_body, out_shape=(pltpu.VMEM((ORDER, ORDER), F32), p...]
where the time goes in v3:
time: 48.9 us; the launch traced here: 48.7 us
  Pallas kernels  47.5 us (97%)
  between operations  1.28 us (3%)
    pallas_call x1, Pallas kernels, per_device(): pl.pallas_call(reduce_body, out_shape=(pltpu.VMEM((ORDER, ORDER), F32), p...  37.6 us
    pallas_call x1, Pallas kernels, per_device(): pl.pallas_call(finish_body, out_shape=(jax.ShapeDtypeStruct((row_count, O...  9.83 us

profile of v3, /device:TPU:1, one launch (start us, length us, event | category | flops | bytes accessed | tf_op | source)
XLA Modules:
  0.0 48.7 jit_solution(4768574660038914100)
XLA Ops:
  1.3 37.6 %reduce_sums.1 = (f32[256,256]{1,0:T(8,128)S(1)}, f32[512,256]{1,0:T(8,128)S(1)}) custom-call(f32[512,256]{1,0:T(8,128)} %refs_0_.1, f32[1,512]{1,0:T(1,128)} %bitcast.1, s32[1]{0:T(128)S(6)} %copy.7.refs_2_, f32[64,512]{1,0:T(8,128)} %refs_3_.1), custom_call_target="tpu_custom_call" | custom-call | tf_op jit(solution)/shard_map/reduce_sums/pallas_call | solution.py:458
  38.9 9.8 %factor_apply.1 = (f32[512,256]{1,0:T(8,128)}, f32[256,256]{1,0:T(8,128)}, f32[64,256]{1,0:T(8,128)}) custom-call(f32[256,256]{1,0:T(8,128)S(1)} %get-tuple-element.5.refs_0_, f32[512,256]{1,0:T(8,128)S(1)} %get-tuple-element.6.refs_1_), custom_call_target="tpu_custom_call" | custom-call | tf_op jit(solution)/shard_map/factor_apply/pallas_call | solution.py:495

commit v4 on v3

--- a/solution.py
+++ b/solution.py
@@ -14,6 +14,7 @@
 TILE = 8
 TILES = ORDER // TILE
 PANEL = 8
+AHEAD = 2
 XS = 4
 YS = 4
 CORES = 2
@@ -24,8 +25,11 @@
 
 def plane_offsets():
     places = [(dx, dy) for dx in range(XS) for dy in range(YS)]
-    hops = lambda place: sum(min(d, 4 - d) for d in place)
     return sorted(places, key=hops, reverse=True)[:-1]
+
+
+def hops(offset):
+    return sum(min(d, size - d) for d, size in zip(offset, (XS, YS)))
 
 
 def reduce_kernel(
@@ -227,28 +231,46 @@
             device_id_type=MESH,
         )
 
-    def cross_copy(place):
+    def other_core_copy(other):
         return pltpu.make_async_remote_copy(
-            src_ref=full.at[own_tile(place), :],
-            dst_ref=full.at[own_tile(place), :],
-            send_sem=cross_send.at[place],
-            recv_sem=cross_recv.at[place],
-            device_id=pair_id(),
+            src_ref=full.at[own_tile(me), :],
+            dst_ref=full.at[own_tile(me), :],
+            send_sem=cross_send.at[other],
+            recv_sem=cross_recv.at[me],
+            device_id=(z * XS + other // YS, other % YS * CORES + 1 - core),
             device_id_type=MESH,
         )
 
+    cross_pair = pltpu.make_async_remote_copy(
+        src_ref=full.at[own_tile(me), :],
+        dst_ref=full.at[own_tile(me), :],
+        send_sem=cross_send.at[me],
+        recv_sem=cross_recv.at[me],
+        device_id=pair_id(),
+        device_id_type=MESH,
+    )
     for other in targets:
         full_copy(other).start()
-    cross_copy(me).start()
+        other_core_copy(other).start()
+    cross_pair.start()
+
+    def arrived(which, place, sems):
+        tile = full.at[
+            pl.ds(pl.multiple_of(which * HALF + place * TILE, TILE), TILE), :
+        ]
+        pltpu.make_async_copy(tile, tile, sems.at[place]).wait()
+
+    arrived(1 - core, me, cross_recv)
     for other in sources:
-        tile = full.at[own_tile(other), :]
-        pltpu.make_async_copy(tile, tile, full_recv.at[other]).wait()
-        cross_copy(other).start()
+        arrived(core, other, full_recv)
+        arrived(1 - core, other, cross_recv)
+    cross_pair.wait_send()
 
     def drain(step, carry):
         other = (me + step) % PLANE
         plane_copy(other).wait_send()
         full_copy(other).wait_send()
+        other_core_copy(other).wait_send()
         return carry
 
     lax.fori_loop(1, PLANE, drain, 0)
@@ -259,15 +281,6 @@
 
     lax.fori_loop(1, DEPTH, drain_depth, 0)
 
-    def wait_cross(place, carry):
-        cross_copy(place).wait_send()
-        tile = full.at[
-            pl.ds(pl.multiple_of((1 - core) * HALF + place * TILE, TILE), TILE), :
-        ]
-        pltpu.make_async_copy(tile, tile, cross_recv.at[place]).wait()
-        return carry
-
-    lax.fori_loop(0, PLANE, wait_cross, 0)
     out_ref[...] = full[...]
 
 
@@ -294,11 +307,11 @@
         half, low = divmod(TILE * t, HALF)
         rows_t = slice(TILE * t, TILE * t + TILE)
         current = [work[rows_t, 0:HALF], work[rows_t, HALF:ORDER]]
-        if t % PANEL == 0:
+        if t == 0:
             diag = [lane_spread(current[half], low + j) for j in range(TILE)]
         unit = jnp.where(lane == low + row_in, 1.0, 0.0)
         inside = (lane >= low) & (lane < low + TILE)
-        last = t == end - 1
+        last = t == TILES - 1
         if not last:
             rows_n = slice(TILE * t + TILE, TILE * t + 2 * TILE)
             after = [work[rows_n, 0:HALF], work[rows_n, HALF:ORDER]]
@@ -353,9 +366,10 @@
             work[rows_n, 0:HALF] = after[0]
             work[rows_n, HALF:ORDER] = after[1]
             diag = diag_n
-            rest = range(t + 2, end)
+            stop = min(end + AHEAD, TILES)
+            rest = range(t + 2, stop)
             if len(rest) > 0:
-                halves = range((TILE * t + 2 * TILE) // HALF, (TILE * end - 1) // HALF + 1)
+                halves = range((TILE * t + 2 * TILE) // HALF, (TILE * stop - 1) // HALF + 1)
                 turned = {i: jnp.transpose(done[i]) for i in halves}
                 tiles = {}
                 for s in rest:
@@ -373,9 +387,9 @@
                     rows_s = slice(TILE * s, TILE * s + TILE)
                     work[rows_s, 0:HALF] = tiles[s][0]
                     work[rows_s, HALF:ORDER] = tiles[s][1]
-        elif end < TILES:
-            reached = TILE * end
-            first = reached - TILE * PANEL
+        if t == end - 1 and end + AHEAD < TILES:
+            reached = TILE * (end + AHEAD)
+            first = TILE * (end - PANEL)
             turned = jnp.transpose(panel_rows[...])
             update = jnp.dot(
                 turned[reached:, :],
@@ -384,7 +398,7 @@
                 preferred_element_type=F32,
             )
             place = lax.broadcasted_iota(jnp.int32, (ORDER - reached, ORDER), 1)
-            in_panel = (place >= first) & (place < reached)
+            in_panel = (place >= first) & (place < TILE * end)
             work[reached:, :] = jnp.where(in_panel, 0.0, work[reached:, :]) - update
 
 

time: 48.9 us -> 47.9 us (0.980)
  Pallas kernels: 47.5 us -> 46.4 us
    pallas_call x1, Pallas kernels: 37.6 us -> 37 us  [per_device(): pl.pallas_call(reduce_body, out_shape=(pltpu.VMEM((ORDER, ORDER), F32), p...]
where the time goes in v4:
time: 47.9 us; the launch traced here: 47.7 us
  Pallas kernels  46.4 us (97%)
  between operations  1.28 us (3%)
    pallas_call x1, Pallas kernels, per_device(): pl.pallas_call(reduce_body, out_shape=(pltpu.VMEM((ORDER, ORDER), F32), p...  37 us
    pallas_call x1, Pallas kernels, per_device(): pl.pallas_call(finish_body, out_shape=(jax.ShapeDtypeStruct((row_count, O...  9.42 us

profile of v4, /device:TPU:1, one launch (start us, length us, event | category | flops | bytes accessed | tf_op | source)
XLA Modules:
  0.0 47.7 jit_solution(16310460730489309196)
XLA Ops:
  1.3 37.0 %reduce_sums.1 = (f32[256,256]{1,0:T(8,128)S(1)}, f32[512,256]{1,0:T(8,128)S(1)}) custom-call(f32[512,256]{1,0:T(8,128)} %refs_0_.1, f32[1,512]{1,0:T(1,128)} %bitcast.1, s32[1]{0:T(128)S(6)} %copy.7.refs_2_, f32[64,512]{1,0:T(8,128)} %refs_3_.1), custom_call_target="tpu_custom_call" | custom-call | tf_op jit(solution)/shard_map/reduce_sums/pallas_call | solution.py:472
  38.3 9.4 %factor_apply.1 = (f32[512,256]{1,0:T(8,128)}, f32[256,256]{1,0:T(8,128)}, f32[64,256]{1,0:T(8,128)}) custom-call(f32[256,256]{1,0:T(8,128)S(1)} %get-tuple-element.5.refs_0_, f32[512,256]{1,0:T(8,128)S(1)} %get-tuple-element.6.refs_1_), custom_call_target="tpu_custom_call" | custom-call | tf_op jit(solution)/shard_map/factor_apply/pallas_call | solution.py:509

commit v5 on v4

--- a/solution.py
+++ b/solution.py
@@ -52,14 +52,8 @@
     load_sems,
     relay_sems,
     pair_sems,
-    plane_send,
-    plane_recv,
-    depth_send,
-    depth_recv,
-    full_send,
-    full_recv,
-    cross_send,
-    cross_recv,
+    send_sems,
+    recv_sems,
 ):
     cells = lax.axis_index("cells")
     sub = lax.axis_index("sub")
@@ -83,6 +77,10 @@
         (x + XS - dx) % XS * YS + (y + YS - dy) % YS
         for dx, dy in reversed(plane_offsets())
     ]
+
+    def settle(sem, tiles):
+        part = full.at[pl.ds(0, tiles * TILE), :]
+        pltpu.make_async_copy(part, part, sem).wait()
 
     def signal(sem, device):
         pl.semaphore_signal(sem, inc=1, device_id=device, device_id_type=MESH)
@@ -166,8 +164,8 @@
         return pltpu.make_async_remote_copy(
             src_ref=pair_buf.at[tile_of(other), :],
             dst_ref=plane_buf.at[me],
-            send_sem=plane_send.at[other],
-            recv_sem=plane_recv.at[me],
+            send_sem=send_sems.at[0],
+            recv_sem=recv_sems.at[0],
             device_id=plane_id(other),
             device_id_type=MESH,
         )
@@ -176,11 +174,9 @@
         plane_copy(other).start()
     pl.semaphore_wait(relay_sems.at[1], 2)
     relay(2)
+    settle(recv_sems.at[0], PLANE - 1)
     total = pair_buf[tile_of(me), :]
     for other in sources:
-        pltpu.make_async_copy(
-            plane_buf.at[other], plane_buf.at[other], plane_recv.at[other]
-        ).wait()
         total = total + plane_buf[other]
 
     depth_buf[z] = total
@@ -189,29 +185,19 @@
         return pltpu.make_async_remote_copy(
             src_ref=depth_buf.at[z],
             dst_ref=depth_buf.at[z],
-            send_sem=depth_send.at[other],
-            recv_sem=depth_recv.at[z],
+            send_sem=send_sems.at[1],
+            recv_sem=recv_sems.at[1],
             device_id=depth_id(other),
             device_id_type=MESH,
         )
 
-    def start_depth(step, carry):
-        far = DEPTH // 2
-        near = (step + 1) // 2 * (1 - step % 2 * 2)
-        depth_copy((z + DEPTH + far - near) % DEPTH).start()
-        return carry
-
     pl.semaphore_wait(relay_sems.at[2], 2)
-    lax.fori_loop(0, DEPTH - 1, start_depth, 0)
-
-    def wait_depth(step, carry):
-        other = (z + step) % DEPTH
-        pltpu.make_async_copy(
-            depth_buf.at[other], depth_buf.at[other], depth_recv.at[other]
-        ).wait()
-        return carry
-
-    lax.fori_loop(1, DEPTH, wait_depth, 0)
+    for step in range(DEPTH // 2, 0, -1):
+        depth_copy((z + step) % DEPTH).start()
+        if step < DEPTH // 2:
+            depth_copy((z + DEPTH - step) % DEPTH).start()
+    settle(send_sems.at[0], PLANE - 1)
+    settle(recv_sems.at[1], DEPTH - 1)
     summed = depth_buf[0]
     for place in range(1, DEPTH):
         summed = summed + depth_buf[place]
@@ -221,66 +207,23 @@
 
     full[own_tile(me), :] = summed
 
-    def full_copy(other):
+    def full_copy(place, which):
         return pltpu.make_async_remote_copy(
             src_ref=full.at[own_tile(me), :],
             dst_ref=full.at[own_tile(me), :],
-            send_sem=full_send.at[other],
-            recv_sem=full_recv.at[me],
-            device_id=plane_id(other),
+            send_sem=send_sems.at[2],
+            recv_sem=recv_sems.at[2],
+            device_id=(z * XS + place // YS, place % YS * CORES + which),
             device_id_type=MESH,
         )
 
-    def other_core_copy(other):
-        return pltpu.make_async_remote_copy(
-            src_ref=full.at[own_tile(me), :],
-            dst_ref=full.at[own_tile(me), :],
-            send_sem=cross_send.at[other],
-            recv_sem=cross_recv.at[me],
-            device_id=(z * XS + other // YS, other % YS * CORES + 1 - core),
-            device_id_type=MESH,
-        )
-
-    cross_pair = pltpu.make_async_remote_copy(
-        src_ref=full.at[own_tile(me), :],
-        dst_ref=full.at[own_tile(me), :],
-        send_sem=cross_send.at[me],
-        recv_sem=cross_recv.at[me],
-        device_id=pair_id(),
-        device_id_type=MESH,
-    )
     for other in targets:
-        full_copy(other).start()
-        other_core_copy(other).start()
-    cross_pair.start()
-
-    def arrived(which, place, sems):
-        tile = full.at[
-            pl.ds(pl.multiple_of(which * HALF + place * TILE, TILE), TILE), :
-        ]
-        pltpu.make_async_copy(tile, tile, sems.at[place]).wait()
-
-    arrived(1 - core, me, cross_recv)
-    for other in sources:
-        arrived(core, other, full_recv)
-        arrived(1 - core, other, cross_recv)
-    cross_pair.wait_send()
-
-    def drain(step, carry):
-        other = (me + step) % PLANE
-        plane_copy(other).wait_send()
-        full_copy(other).wait_send()
-        other_core_copy(other).wait_send()
-        return carry
-
-    lax.fori_loop(1, PLANE, drain, 0)
-
-    def drain_depth(step, carry):
-        depth_copy((z + step) % DEPTH).wait_send()
-        return carry
-
-    lax.fori_loop(1, DEPTH, drain_depth, 0)
-
+        full_copy(other, core).start()
+        full_copy(other, 1 - core).start()
+    full_copy(me, 1 - core).start()
+    settle(send_sems.at[1], DEPTH - 1)
+    settle(recv_sems.at[2], CORES * PLANE - 1)
+    settle(send_sems.at[2], CORES * PLANE - 1)
     out_ref[...] = full[...]
 
 
@@ -490,14 +433,8 @@
             dma((4,)),
             pltpu.SemaphoreType.REGULAR((len(RELAYS),)),
             dma((2,)),
-            dma((PLANE,)),
-            dma((PLANE,)),
-            dma((DEPTH,)),
-            dma((DEPTH,)),
-            dma((PLANE,)),
-            dma((PLANE,)),
-            dma((PLANE,)),
-            dma((PLANE,)),
+            dma((3,)),
+            dma((3,)),
         ],
         compiler_params=pltpu.CompilerParams(collective_id=0, has_side_effects=True),
         name="reduce_sums",

time: 47.9 us -> 46.5 us (0.971)
  Pallas kernels: 46.4 us -> 45.1 us
    pallas_call x1, Pallas kernels: 37 us -> 35.7 us  [per_device(): pl.pallas_call(reduce_body, out_shape=(pltpu.VMEM((ORDER, ORDER), F32), p...]
where the time goes in v5:
time: 46.5 us; the launch traced here: 46.4 us
  Pallas kernels  45.1 us (97%)
  between operations  1.28 us (3%)
    pallas_call x1, Pallas kernels, per_device(): pl.pallas_call(reduce_body, out_shape=(pltpu.VMEM((ORDER, ORDER), F32), p...  35.7 us
    pallas_call x1, Pallas kernels, per_device(): pl.pallas_call(finish_body, out_shape=(jax.ShapeDtypeStruct((row_count, O...  9.42 us

profile of v5, /device:TPU:1, one launch (start us, length us, event | category | flops | bytes accessed | tf_op | source)
XLA Modules:
  0.0 46.4 jit_solution(16190906598031842135)
XLA Ops:
  1.3 35.7 %reduce_sums.1 = (f32[256,256]{1,0:T(8,128)S(1)}, f32[512,256]{1,0:T(8,128)S(1)}) custom-call(f32[512,256]{1,0:T(8,128)} %refs_0_.1, f32[1,512]{1,0:T(1,128)} %bitcast.1, s32[1]{0:T(128)S(6)} %copy.7.refs_2_, f32[64,512]{1,0:T(8,128)} %refs_3_.1), custom_call_target="tpu_custom_call" | custom-call | tf_op jit(solution)/shard_map/reduce_sums/pallas_call | solution.py:415
  36.9 9.4 %factor_apply.1 = (f32[512,256]{1,0:T(8,128)}, f32[256,256]{1,0:T(8,128)}, f32[64,256]{1,0:T(8,128)}) custom-call(f32[256,256]{1,0:T(8,128)S(1)} %get-tuple-element.5.refs_0_, f32[512,256]{1,0:T(8,128)S(1)} %get-tuple-element.6.refs_1_), custom_call_target="tpu_custom_call" | custom-call | tf_op jit(solution)/shard_map/factor_apply/pallas_call | solution.py:446

commit v6 on v5

--- a/solution.py
+++ b/solution.py
@@ -14,7 +14,7 @@
 TILE = 8
 TILES = ORDER // TILE
 PANEL = 8
-AHEAD = 2
+AHEAD = 3
 XS = 4
 YS = 4
 CORES = 2
@@ -387,8 +387,8 @@
     coef[...] = apply(cross) / F32(root_total)
     copies.append(pltpu.make_async_copy(coef, coef_hbm, sems.at[1]))
     copies[1].start()
-    for part in range(basis.shape[0] // HALF):
-        rows = slice(HALF * part, HALF * part + HALF)
+    for part in range(basis.shape[0] // ORDER):
+        rows = slice(ORDER * part, ORDER * part + ORDER)
         basis[rows, :] = apply(weighted[rows, :])
         copies.append(
             pltpu.make_async_copy(
@@ -459,7 +459,7 @@
             pltpu.VMEM((TILE * PANEL, ORDER), F32),
             pltpu.VMEM((row_count, ORDER), F32),
             pltpu.VMEM((count, ORDER), F32),
-            dma((2 + row_count // HALF,)),
+            dma((2 + row_count // ORDER,)),
         ],
         name="factor_apply",
     )(

time: 46.5 us -> 45.7 us (0.983)
  Pallas kernels: 45.1 us -> 44.3 us
    pallas_call x1, Pallas kernels: 9.42 us -> 8.61 us  [per_device(): pl.pallas_call(finish_body, out_shape=(jax.ShapeDtypeStruct((row_count, O...]
where the time goes in v6:
time: 45.7 us; the launch traced here: 45.6 us
  Pallas kernels  44.3 us (97%)
  between operations  1.28 us (3%)
    pallas_call x1, Pallas kernels, per_device(): pl.pallas_call(reduce_body, out_shape=(pltpu.VMEM((ORDER, ORDER), F32), p...  35.7 us
    pallas_call x1, Pallas kernels, per_device(): pl.pallas_call(finish_body, out_shape=(jax.ShapeDtypeStruct((row_count, O...  8.61 us

profile of v6, /device:TPU:1, one launch (start us, length us, event | category | flops | bytes accessed | tf_op | source)
XLA Modules:
  0.0 45.6 jit_solution(5087600147025874995)
XLA Ops:
  1.3 35.7 %reduce_sums.1 = (f32[256,256]{1,0:T(8,128)S(1)}, f32[512,256]{1,0:T(8,128)S(1)}) custom-call(f32[512,256]{1,0:T(8,128)} %refs_0_.1, f32[1,512]{1,0:T(1,128)} %bitcast.1, s32[1]{0:T(128)S(6)} %copy.7.refs_2_, f32[64,512]{1,0:T(8,128)} %refs_3_.1), custom_call_target="tpu_custom_call" | custom-call | tf_op jit(solution)/shard_map/reduce_sums/pallas_call | solution.py:415
  36.9 8.6 %factor_apply.1 = (f32[512,256]{1,0:T(8,128)}, f32[256,256]{1,0:T(8,128)}, f32[64,256]{1,0:T(8,128)}) custom-call(f32[256,256]{1,0:T(8,128)S(1)} %get-tuple-element.5.refs_0_, f32[512,256]{1,0:T(8,128)S(1)} %get-tuple-element.6.refs_1_), custom_call_target="tpu_custom_call" | custom-call | tf_op jit(solution)/shard_map/factor_apply/pallas_call | solution.py:446
